TPU v7x, 32 devices: a whole 2x2x4 slice. The times are simulated.
32 devices in a mesh: tm: 16 (over z, y, x), space: 2 (over core).
Axes of the slice: x: 2, y: 2, z: 4, core: 2. Of those that a mesh axis runs over, the one named last changes fastest.
Arguments:
- features: bfloat16 [16, 16, 16, 256], P('tm', 'space'), may hold values from -6 to 6
- masks: int32 [16, 16, 16], P('tm', 'space'), may hold values from 0 to 1
- w_pix: bfloat16 [256, 256], replicated, may hold values from -0.375 to 0.375
- mask_embed: bfloat16 [256], replicated, may hold values from -4 to 4
- w_conv: bfloat16 [3, 3, 256, 256], replicated, may hold values from -0.125 to 0.125
- w_out: bfloat16 [256, 64], replicated, may hold values from -0.375 to 0.375
- w_ptr: bfloat16 [256, 256], replicated, may hold values from -0.375 to 0.375
- w_query: bfloat16 [256, 256], replicated, may hold values from -1 to 1
- w_key: bfloat16 [64, 256], replicated, may hold values from -0.75 to 0.75
- w_value: bfloat16 [64, 256], replicated, may hold values from -0.75 to 0.75
- w_proj: bfloat16 [256, 256], replicated, may hold values from -0.375 to 0.375
- mem_tpos: bfloat16 [3, 64], replicated, may hold values from -120 to 120
- ptr_tpos: bfloat16 [16, 256], replicated, may hold values from -4 to 4
- empty_memory: bfloat16 [64], replicated, may hold values from -4 to 4
Outputs:
- attended: bfloat16 [16, 16, 16, 256], P('tm', 'space')
- memory: bfloat16 [16, 16, 1024], P('tm', 'space')
- pointers: bfloat16 [16, 256], P('tm')
All inputs are finite; a program needn't handle non-finite values.
Results may differ from a plain program's by a relative error of at most 0.015.
The roundings to bfloat16 on the way count: a program that leaves them out, or rounds other values in their place, can miss the bound.
Values may be sent and summed in bfloat16 or wider, within the bound.
A program may use at most 128 MiB of HBM per device.

v0:
```python
import jax
import jax.numpy as jnp
from jax import lax
from jax.sharding import PartitionSpec as P

MEMS = 3
POINTERS = 16


def from_behind(block, axis, distance):
    devices = range(lax.axis_size(axis))
    route = [(i - distance, i) for i in devices if i - distance in devices]
    return lax.ppermute(block, axis, route)


def with_halo(block, sides, width):
    for axis, dim in sides:
        count = lax.axis_size(axis)
        forward = [(i, i + 1) for i in range(count - 1)]
        backward = [(target, source) for source, target in forward]
        low = lax.ppermute(
            lax.slice_in_dim(block, block.shape[dim] - width, None, axis=dim), axis, forward
        )
        high = lax.ppermute(lax.slice_in_dim(block, 0, width, axis=dim), axis, backward)
        block = jnp.concatenate([low, block, high], axis=dim)
    return block


def fetch_earlier(carried, hop_count):
    pieces = []
    for step_index in range(hop_count):
        pieces.append(from_behind(carried, "tm", step_index + 1))
    return jnp.concatenate(pieces[::-1], axis=0)


def attend(query, blocks):
    scores = []
    row_top = None
    for key_rows, value_rows, is_valid in blocks:
        block_scores = lax.dot_general(
            query, key_rows, (((1,), (1,)), ((), ())), preferred_element_type=jnp.float32
        )
        block_scores = jnp.where(is_valid, block_scores, -jnp.inf)
        scores.append(block_scores)
        block_top = jnp.max(block_scores, axis=1, keepdims=True)
        row_top = block_top if row_top is None else jnp.maximum(row_top, block_top)
    row_total = jnp.zeros_like(row_top)
    for block_scores in scores:
        row_total = row_total + jnp.sum(jnp.exp(block_scores - row_top), axis=1, keepdims=True)
    mixed_sum = jnp.zeros((query.shape[0], blocks[0][1].shape[1]), jnp.float32)
    for block_scores, block in zip(scores, blocks):
        weights = (jnp.exp(block_scores - row_top) / row_total).astype(jnp.bfloat16)
        mixed_sum = mixed_sum + jnp.dot(weights, block[1], preferred_element_type=jnp.float32)
    return mixed_sum.astype(jnp.bfloat16)


def body(
    features,
    masks,
    w_pix,
    mask_embed,
    w_conv,
    w_out,
    w_ptr,
    w_query,
    w_key,
    w_value,
    w_proj,
    mem_tpos,
    ptr_tpos,
    empty_memory,
):
    frames_dev, rows_dev, columns, model_dim = features.shape
    mem_dim = w_key.shape[0]
    ptr_tok = model_dim // mem_dim
    band_tokens = rows_dev * columns
    flat_rows = features.reshape(frames_dev * band_tokens, model_dim)
    mask_rows = masks.reshape(frames_dev * band_tokens, 1).astype(jnp.float32)
    joined_map = (
        jnp.dot(flat_rows, w_pix, preferred_element_type=jnp.float32)
        + mask_rows * mask_embed.astype(jnp.float32)
    ).astype(jnp.bfloat16)
    joined_map = joined_map.reshape(frames_dev, rows_dev, columns, model_dim)
    padded = with_halo(joined_map, (("space", 1),), 1)
    padded = jnp.pad(padded, ((0, 0), (0, 0), (1, 1), (0, 0)))
    conv_sum = jnp.zeros((frames_dev * band_tokens, model_dim), jnp.float32)
    for row_tap in range(3):
        for col_tap in range(3):
            window_rows = padded[
                :, row_tap : row_tap + rows_dev, col_tap : col_tap + columns, :
            ].reshape(-1, model_dim)
            conv_sum = conv_sum + jnp.dot(
                window_rows, w_conv[row_tap, col_tap], preferred_element_type=jnp.float32
            )
    hidden = jax.nn.gelu(conv_sum, approximate=True).astype(jnp.bfloat16)
    memory = jnp.dot(hidden, w_out, preferred_element_type=jnp.float32).astype(jnp.bfloat16)
    memory = memory.reshape(frames_dev, rows_dev, columns * mem_dim)
    band_mask = masks.reshape(frames_dev, band_tokens).astype(jnp.bfloat16)
    partial_value = jnp.einsum(
        "ft,ftd->fd",
        band_mask,
        features.reshape(frames_dev, band_tokens, model_dim),
        preferred_element_type=jnp.float32,
    )
    pooled = lax.psum(partial_value, "space")
    normed = (pooled * lax.rsqrt(jnp.mean(pooled * pooled, axis=1, keepdims=True) + 1e-06)).astype(
        jnp.bfloat16
    )
    pointers = jnp.dot(normed, w_ptr, preferred_element_type=jnp.float32).astype(jnp.bfloat16)
    all_pointers = lax.all_gather(pointers, "tm", axis=0, tiled=True)
    hop_count = (MEMS + frames_dev - 1) // frames_dev
    carried = lax.all_gather(memory, "space", axis=1, tiled=True)
    history = jnp.concatenate(
        [fetch_earlier(carried, hop_count), carried[: frames_dev - 1]], axis=0
    )
    grid_tokens = columns * columns
    hist_frames = history.shape[0]
    history = history.reshape(hist_frames, grid_tokens, mem_dim)
    hist_values = jnp.dot(
        history.reshape(-1, mem_dim), w_value, preferred_element_type=jnp.float32
    ).astype(jnp.bfloat16)
    hist_values = hist_values.reshape(hist_frames, grid_tokens, model_dim)
    tpos_keys = jnp.dot(mem_tpos, w_key, preferred_element_type=jnp.float32)
    ptr_tpos_keys = jnp.dot(
        ptr_tpos[::-1].reshape(POINTERS * ptr_tok, mem_dim),
        w_key,
        preferred_element_type=jnp.float32,
    )
    null_key = jnp.dot(
        empty_memory.reshape(1, mem_dim), w_key, preferred_element_type=jnp.float32
    ).astype(jnp.bfloat16)
    null_value = jnp.dot(
        empty_memory.reshape(1, mem_dim), w_value, preferred_element_type=jnp.float32
    ).astype(jnp.bfloat16)
    padded_ptr = jnp.concatenate(
        [jnp.zeros((POINTERS, model_dim), jnp.bfloat16), all_pointers], axis=0
    )
    ptr_offsets = jnp.repeat(jnp.arange(POINTERS, dtype=jnp.int32) - POINTERS, ptr_tok)
    features_f = features.reshape(frames_dev, band_tokens, model_dim).astype(jnp.float32)
    first_frame = lax.axis_index("tm") * frames_dev
    frame = first_frame + 0
    rows_f = features_f[0]
    centred = rows_f - jnp.mean(rows_f, axis=1, keepdims=True)
    query_in = (
        centred * lax.rsqrt(jnp.mean(centred * centred, axis=1, keepdims=True) + 1e-05)
    ).astype(jnp.bfloat16)
    query = (
        jnp.dot(query_in, w_query, preferred_element_type=jnp.float32) * model_dim ** (-0.5)
    ).astype(jnp.bfloat16)
    blocks = []
    for distance in range(1, MEMS + 1):
        slot_index = hop_count * frames_dev - distance
        key_rows = (
            jnp.dot(history[slot_index], w_key, preferred_element_type=jnp.float32)
            + tpos_keys[distance - 1]
        ).astype(jnp.bfloat16)
        blocks.append((key_rows, hist_values[slot_index], frame - distance >= 0))
    window = lax.dynamic_slice_in_dim(padded_ptr, frame, POINTERS, 0)
    ptr_tokens = window.reshape(POINTERS * ptr_tok, mem_dim)
    ptr_keys = (
        jnp.dot(ptr_tokens, w_key, preferred_element_type=jnp.float32) + ptr_tpos_keys
    ).astype(jnp.bfloat16)
    ptr_values = jnp.dot(ptr_tokens, w_value, preferred_element_type=jnp.float32).astype(
        jnp.bfloat16
    )
    extra_valid = jnp.concatenate([frame + ptr_offsets >= 0, jnp.ones((1,), bool)], axis=0)
    blocks.append(
        (
            jnp.concatenate([ptr_keys, null_key], axis=0),
            jnp.concatenate([ptr_values, null_value], axis=0),
            extra_valid[None, :],
        )
    )
    mixed_rows = attend(query, blocks)
    outputs = [
        (rows_f + jnp.dot(mixed_rows, w_proj, preferred_element_type=jnp.float32)).astype(
            jnp.bfloat16
        )
    ]
    attended = jnp.stack(outputs, axis=0).reshape(frames_dev, rows_dev, columns, model_dim)
    return (attended, memory, pointers)


def solution(mesh):
    return jax.shard_map(
        body,
        mesh=mesh,
        in_specs=(
            P("tm", "space", None, None),
            P("tm", "space", None),
            P(),
            P(),
            P(),
            P(),
            P(),
            P(),
            P(),
            P(),
            P(),
            P(),
            P(),
            P(),
        ),
        out_specs=(P("tm", "space", None, None), P("tm", "space", None), P("tm", None)),
        check_vma=False,
    )
```

profile of v0, /device:TPU:24, one launch (start us, length us, event | category | flops | bytes accessed | tf_op | source)
XLA Modules:
  0.0 78.9 jit_solution(8171158523613113094)
XLA Ops:
  0.6 0.0 copy-start
  0.7 0.0 copy-start.7
  0.7 0.0 copy-start.4
  0.7 0.7 convert_element_type.111
  1.4 0.8 convert_bitcast_fusion
  2.2 0.1 convert_element_type.110
  2.3 1.0 %fusion.12 = bf16[128,256]{1,0:T(8,128)(2,1)S(1)} fusion(bf16[128,256]{1,0:T(8,128)(2,1)} %bitcast.107, bf16[256,256]{1,0:T(8,128)(2,1)S(1)} %copy-done, f32[256]{0:T(256)S(1)} %convert_element_type.111, f32[128]{0:T(128)S(1)} %convert_element_type.110), kind=kOutput, calls=%fused_computation.29 | convolution fusion | flops 16875520 | bytes 263680 | tf_op jit(solution)/shard_map/dot_general | solution.py:80
  3.3 1.3 %collective-permute-start.1 = (bf16[1,1,16,256]{3,2,1,0:T(8,128)(2,1)S(1)}, bf16[1,1,16,256]{3,2,1,0:T(8,128)(2,1)S(1)}, u32[]{:S(2)}, u32[]{:S(2)}) collective-permute-start(bf16[1,1,16,256]{3,2,1,0:T(8,128)(2,1)S(1)} %get-tuple-element.15), channel_id=1, source_target_pairs={{1,0},{3,2},{5,4},{7,6},{9,8},{11,10},{13,12},{15,14},{17,16},{19,... | collective-permute-start | bytes 24584 | tf_op jit(solution)/shard_map/ppermute | solution.py:24
  4.6 3.0 %collective-permute-start = (bf16[1,1,16,256]{3,2,1,0:T(8,128)(2,1)S(1)}, bf16[1,1,16,256]{3,2,1,0:T(8,128)(2,1)S(1)}, u32[]{:S(2)}, u32[]{:S(2)}) collective-permute-start(bf16[1,1,16,256]{3,2,1,0:T(8,128)(2,1)S(1)} %get-tuple-element.14), channel_id=1, source_target_pairs={{0,1},{2,3},{4,5},{6,7},{8,9},{10,11},{12,13},{14,15},{16,17},{18,... | collective-permute-start | bytes 24584 | tf_op jit(solution)/shard_map/ppermute | solution.py:21
  7.6 0.9 %convert_reduce_fusion = f32[8,16]{1,0:T(8,128)S(1)} fusion(bf16[1,8,16,256]{3,2,1,0:T(8,128)(2,1)} %param.14), kind=kLoop, calls=%fused_computation.42 | loop fusion | flops 65408 | bytes 66048 | tf_op jit(solution)/shard_map/reduce_sum | solution.py:143
  8.6 1.1 %fusion.22 = f32[8,16]{1,0:T(8,128)S(1)} fusion(bf16[1,8,16,256]{3,2,1,0:T(8,128)(2,1)} %param.14, f32[8,16]{1,0:T(8,128)S(1)} %broadcast_multiply_fusion), kind=kLoop, calls=%fused_computation.50 | loop fusion | flops 130944 | bytes 66560 | tf_op jit(solution)/shard_map/reduce_sum | solution.py:145
  9.7 0.1 div.40
  9.8 0.1 rsqrt.16
  9.8 0.9 %fusion.117 = f32[3,256]{1,0:T(4,128)S(1)} fusion(bf16[3,64]{1,0:T(4,128)(2,1)} %param.25, bf16[64,256]{1,0:T(8,128)(2,1)} %param.22), kind=kOutput, calls=%fused_computation.157 | convolution fusion | flops 98304 | bytes 36224 | tf_op jit(solution)/shard_map/dot_general | solution.py:123
  10.8 0.9 %fusion.100 = f32[1,256]{1,0:T(1,128)S(1)} fusion(bf16[64,256]{1,0:T(8,128)(2,1)} %param.22, bf16[64]{0:T(256)(128)(2,1)} %param.27), kind=kOutput, calls=%fused_computation.138 | convolution fusion | flops 32768 | bytes 33920 | tf_op jit(solution)/shard_map/dot_general | solution.py:129
  11.7 1.0 %convolution_bitcast_fusion = f32[1,256]{1,0:T(1,128)S(1)} fusion(bf16[1,8,16,256]{3,2,1,0:T(8,128)(2,1)} %param.14, bf16[8,16,1]{1,0,2:T(8,128)(2,1)S(1)} %get-tuple-element.19), kind=kOutput, calls=%fused_computation.36 | convolution fusion | flops 65536 | bytes 66816 | tf_op jit(solution)/shard_map/ft,ftd->fd/dot_general | solution.py:99
  12.7 2.4 %psum.7 = f32[1,256]{1,0:T(1,128)S(1)} all-reduce(f32[1,256]{1,0:T(1,128)S(1)} %convolution_bitcast_fusion), channel_id=1, replica_groups=mesh['tm'=16,'space'=2] {'space'}, use_global_device_ids=true, to_apply=%region_5.6 | all-reduce | flops 256 | bytes 2048 | tf_op jit(solution)/shard_map/psum | solution.py:105
  15.2 0.6 multiply_reduce_fusion
  16.5 1.0 %fusion.94 = f32[1,256]{1,0:T(1,128)S(1)} fusion(bf16[256,256]{1,0:T(8,128)(2,1)} %param.20, f32[1,256]{1,0:T(1,128)S(1)} %psum.7, f32[]{:T(128)S(6)} %rsqrt.17), kind=kOutput, calls=%fused_computation.131 | convolution fusion | flops 131584 | bytes 133124 | tf_op jit(solution)/shard_map/dot_general | solution.py:109
  17.5 32.6 %all-gather.1 = bf16[16,1,256]{2,1,0:T(2,128)(2,1)S(1)} all-gather(bf16[1,1,256]{2,1,0:T(2,128)(2,1)S(1)} %reshape.203), channel_id=2, replica_groups=mesh['tm'=16,'space'=2] {'tm'}, dimensions={0}, use_global_device_ids=true | all-gather | bytes 8704 | tf_op jit(solution)/shard_map/all_gather | solution.py:110
  50.1 0.1 reshape.200
  50.2 0.9 %fusion.118 = f32[64,256]{1,0:T(8,128)S(1)} fusion(bf16[64,64]{1,0:T(8,128)(2,1)S(1)} %reshape.200, bf16[64,256]{1,0:T(8,128)(2,1)} %param.22), kind=kOutput, calls=%fused_computation.158 | convolution fusion | flops 2097152 | bytes 106496 | tf_op jit(solution)/shard_map/dot_general | solution.py:161
  51.1 0.7 rev.3
  51.8 0.1 reshape.201
  51.9 0.1 broadcast_in_dim.21
  52.0 0.1 ge.24
  52.1 0.9 %convolution_convert_fusion.1 = bf16[64,256]{1,0:T(8,128)(2,1)S(1)} fusion(bf16[64,64]{1,0:T(8,128)(2,1)S(1)} %reshape.200, bf16[64,256]{1,0:T(8,128)(2,1)} %param.23), kind=kOutput, calls=%fused_computation.33 | convolution fusion | flops 2113536 | bytes 73728 | tf_op jit(solution)/shard_map/dot_general | solution.py:163
  53.0 0.9 %fusion.14 = bf16[64,256]{1,0:T(8,128)(2,1)S(1)} fusion(f32[64,256]{1,0:T(8,128)S(1)} %fusion.118, bf16[64,64]{1,0:T(8,128)(2,1)S(1)} %reshape.201, bf16[64,256]{1,0:T(8,128)(2,1)} %param.22), kind=kOutput, calls=%fused_computation.32 | convolution fusion | flops 2129920 | bytes 139264 | tf_op jit(solution)/shard_map/dot_general | solution.py:124
  53.9 0.1 pad_add_fusion
  54.0 0.2 fusion.11
  54.2 0.2 fusion.113
  54.4 0.1 fusion.98
  54.6 0.2 fusion.35
  54.8 0.2 fusion.45
  55.0 0.2 convolution_add_fusion.13
  55.1 0.2 convolution_add_fusion.12
  55.3 0.2 convolution_add_fusion.11
  55.5 0.2 convolution_add_fusion.10
  55.7 0.2 convolution_add_fusion.9
  55.8 0.2 convolution_add_fusion.8
  56.0 0.3 convolution_convert_fusion.2
  56.4 0.1 copy.19
  56.5 0.1 reshape.196
  56.6 0.0 copy-start.6
  56.6 1.8 %all_gather.6 = bf16[1,16,1024]{2,1,0:T(8,128)(2,1)S(1)} all-gather(bf16[1,8,1024]{2,1,0:T(8,128)(2,1)S(1)} %reshape.196), channel_id=1, replica_groups=mesh['tm'=16,'space'=2] {'space'}, dimensions={1}, use_global_device_ids=true | all-gather | bytes 49152 | tf_op jit(solution)/shard_map/all_gather | solution.py:112
  58.4 3.4 %collective-permute-start.2 = (bf16[1,16,1024]{2,1,0:T(8,128)(2,1)S(1)}, bf16[1,16,1024]{2,1,0:T(8,128)(2,1)S(1)}, u32[]{:S(2)}, u32[]{:S(2)}) collective-permute-start(bf16[1,16,1024]{2,1,0:T(8,128)(2,1)S(1)} %all_gather.6), channel_id=1, source_target_pairs={{0,2},{2,4},{4,6},{6,8},{8,10},{10,12},{12,14},{14,16},{16,18},{18... | collective-permute-start | bytes 98312 | tf_op jit(solution)/shard_map/ppermute | solution.py:13
  61.9 6.1 %collective-permute-start.3 = (bf16[1,16,1024]{2,1,0:T(8,128)(2,1)S(1)}, bf16[1,16,1024]{2,1,0:T(8,128)(2,1)S(1)}, u32[]{:S(2)}, u32[]{:S(2)}) collective-permute-start(bf16[1,16,1024]{2,1,0:T(8,128)(2,1)S(1)} %all_gather.6), channel_id=1, source_target_pairs={{0,4},{2,6},{4,8},{6,10},{8,12},{10,14},{12,16},{14,18},{16,20},{1... | collective-permute-start | bytes 98312 | tf_op jit(solution)/shard_map/ppermute | solution.py:13
  68.0 1.9 %collective-permute-start.4 = (bf16[1,16,1024]{2,1,0:T(8,128)(2,1)S(1)}, bf16[1,16,1024]{2,1,0:T(8,128)(2,1)S(1)}, u32[]{:S(2)}, u32[]{:S(2)}) collective-permute-start(bf16[1,16,1024]{2,1,0:T(8,128)(2,1)S(1)} %all_gather.6), channel_id=1, source_target_pairs={{0,6},{2,8},{4,10},{6,12},{8,14},{10,16},{12,18},{14,20},{16,22},{... | collective-permute-start | bytes 98312 | tf_op jit(solution)/shard_map/ppermute | solution.py:13
  69.9 0.6 convert_element_type.121
  70.5 4.2 %collective-permute-done.4 = bf16[1,16,1024]{2,1,0:T(8,128)(2,1)S(1)} collective-permute-done((bf16[1,16,1024]{2,1,0:T(8,128)(2,1)S(1)}, bf16[1,16,1024]{2,1,0:T(8,128)(2,1)S(1)}, u32[]{:S(2)}, u32[]{:S(2)}) %collective-permute-start.4) | collective-permute-done | bytes 32800 | tf_op jit(solution)/shard_map/ppermute | solution.py:13
  74.7 0.2 reshape_reshape.3
  74.9 0.2 convolution_convert_fusion
  75.1 0.1 squeeze.49
  75.2 0.4 fusion.115
  75.6 0.1 squeeze.51
  75.8 0.4 fusion.114
  76.2 0.1 squeeze.50
  76.3 0.4 fusion.116
  76.8 0.2 fusion.63
  77.1 0.2 fusion.33
  77.3 0.2 convolution_add_fusion.6
  77.5 0.2 convolution_add_fusion.5
  77.8 0.2 copy-done.5
  78.0 1.0 %fusion.13 = bf16[128,256]{1,0:T(8,128)(2,1)} fusion(bf16[256,256]{1,0:T(8,128)(2,1)S(1)} %copy-done.5, f32[128,256]{1,0:T(8,128)S(1)} %convolution_add_fusion.5, bf16[128,256]{1,0:T(8,128)(2,1)S(1)} %bitcast.109, bf16[1,256]{1,0:T(2,128)(2,1)S(1)} %convert_element_type.132, bf16[64,256]{1,0:T(8,128)(2,1)S(1)} %convolution_convert_fusion.1, ...), kind=kOutput, calls=%fused_computation.30 | convolution fusion | flops 21292416 | bytes 460800 | tf_op jit(solution)/shard_map/dot_general | solution.py:176
  (39 shorter events, 0.3 us)
Async XLA Ops:
  0.6 1.6 %copy-start = (bf16[256,256]{1,0:T(8,128)(2,1)S(1)}, bf16[256,256]{1,0:T(8,128)(2,1)}, u32[]{:S(2)}) copy-start(bf16[256,256]{1,0:T(8,128)(2,1)} %param.16) | copy-start | bytes 393220
  0.6 53.3 %copy-start.2 = (bf16[1,8,16,256]{3,2,1,0:T(8,128)(2,1)S(1)}, bf16[1,8,16,256]{3,2,1,0:T(8,128)(2,1)}, u32[]{:S(2)}) copy-start(bf16[1,8,16,256]{3,2,1,0:T(8,128)(2,1)} %param.14) | copy-start | bytes 196612
  0.7 53.7 %copy-start.7 = (bf16[64]{0:T(256)(128)(2,1)S(1)}, bf16[64]{0:T(256)(128)(2,1)}, u32[]{:S(2)}) copy-start(bf16[64]{0:T(256)(128)(2,1)} %param.27) | copy-start | bytes 388
  0.7 53.7 %copy-start.4 = (bf16[64,256]{1,0:T(8,128)(2,1)S(1)}, bf16[64,256]{1,0:T(8,128)(2,1)}, u32[]{:S(2)}) copy-start(bf16[64,256]{1,0:T(8,128)(2,1)} %param.23) | copy-start | bytes 98308
  0.7 53.3 %copy-start.8 = (bf16[256,256]{1,0:T(8,128)(2,1)S(1)}, bf16[256,256]{1,0:T(8,128)(2,1)}, u32[]{:S(2)}) copy-start(bf16[256,256]{1,0:T(8,128)(2,1)} %param.21) | copy-start | bytes 393220
  3.3 51.2 %collective-permute-start.1 = (bf16[1,1,16,256]{3,2,1,0:T(8,128)(2,1)S(1)}, bf16[1,1,16,256]{3,2,1,0:T(8,128)(2,1)S(1)}, u32[]{:S(2)}, u32[]{:S(2)}) collective-permute-start(bf16[1,1,16,256]{3,2,1,0:T(8,128)(2,1)S(1)} %get-tuple-element.15), channel_id=1, source_target_pairs={{1,0},{3,2},{5,4},{7,6},{9,8},{11,10},{13,12},{15,14},{17,16},{19,... | collective-permute-start | bytes 24584 | tf_op jit(solution)/shard_map/ppermute | solution.py:24
  4.6 49.9 %collective-permute-start = (bf16[1,1,16,256]{3,2,1,0:T(8,128)(2,1)S(1)}, bf16[1,1,16,256]{3,2,1,0:T(8,128)(2,1)S(1)}, u32[]{:S(2)}, u32[]{:S(2)}) collective-permute-start(bf16[1,1,16,256]{3,2,1,0:T(8,128)(2,1)S(1)} %get-tuple-element.14), channel_id=1, source_target_pairs={{0,1},{2,3},{4,5},{6,7},{8,9},{10,11},{12,13},{14,15},{16,17},{18,... | collective-permute-start | bytes 24584 | tf_op jit(solution)/shard_map/ppermute | solution.py:21
  8.6 46.0 %copy-start.3 = (bf16[3,3,256,256]{3,2,1,0:T(8,128)(2,1)S(1)}, bf16[3,3,256,256]{3,2,1,0:T(8,128)(2,1)}, u32[]{:S(2)}) copy-start(bf16[3,3,256,256]{3,2,1,0:T(8,128)(2,1)} %param.18) | copy-start | bytes 3538948
  55.1 0.9 %copy-start.9 = (bf16[256,64]{0,1:T(8,128)(2,1)S(1)}, bf16[256,64]{0,1:T(8,128)(2,1)}, u32[]{:S(2)}) copy-start(bf16[256,64]{0,1:T(8,128)(2,1)} %param.19) | copy-start | bytes 98308
  55.8 19.4 %copy-start.1 = (bf16[64,256]{1,0:T(8,128)(2,1)S(1)}, bf16[64,256]{1,0:T(8,128)(2,1)}, u32[]{:S(2)}) copy-start(bf16[64,256]{1,0:T(8,128)(2,1)} %param.22) | copy-start | bytes 98308
  56.6 20.2 %copy-start.6 = (bf16[1,8,1024]{2,1,0:T(8,128)(2,1)}, bf16[1,8,1024]{2,1,0:T(8,128)(2,1)S(1)}, u32[]{:S(2)}) copy-start(bf16[1,8,1024]{2,1,0:T(8,128)(2,1)S(1)} %reshape.196) | copy-start | bytes 49156
  58.4 12.0 %collective-permute-start.2 = (bf16[1,16,1024]{2,1,0:T(8,128)(2,1)S(1)}, bf16[1,16,1024]{2,1,0:T(8,128)(2,1)S(1)}, u32[]{:S(2)}, u32[]{:S(2)}) collective-permute-start(bf16[1,16,1024]{2,1,0:T(8,128)(2,1)S(1)} %all_gather.6), channel_id=1, source_target_pairs={{0,2},{2,4},{4,6},{6,8},{8,10},{10,12},{12,14},{14,16},{16,18},{18... | collective-permute-start | bytes 98312 | tf_op jit(solution)/shard_map/ppermute | solution.py:13
  61.9 8.6 %collective-permute-start.3 = (bf16[1,16,1024]{2,1,0:T(8,128)(2,1)S(1)}, bf16[1,16,1024]{2,1,0:T(8,128)(2,1)S(1)}, u32[]{:S(2)}, u32[]{:S(2)}) collective-permute-start(bf16[1,16,1024]{2,1,0:T(8,128)(2,1)S(1)} %all_gather.6), channel_id=1, source_target_pairs={{0,4},{2,6},{4,8},{6,10},{8,12},{10,14},{12,16},{14,18},{16,20},{1... | collective-permute-start | bytes 98312 | tf_op jit(solution)/shard_map/ppermute | solution.py:13
  68.0 6.7 %collective-permute-start.4 = (bf16[1,16,1024]{2,1,0:T(8,128)(2,1)S(1)}, bf16[1,16,1024]{2,1,0:T(8,128)(2,1)S(1)}, u32[]{:S(2)}, u32[]{:S(2)}) collective-permute-start(bf16[1,16,1024]{2,1,0:T(8,128)(2,1)S(1)} %all_gather.6), channel_id=1, source_target_pairs={{0,6},{2,8},{4,10},{6,12},{8,14},{10,16},{12,18},{14,20},{16,22},{... | collective-permute-start | bytes 98312 | tf_op jit(solution)/shard_map/ppermute | solution.py:13
  77.0 0.9 %copy-start.5 = (bf16[256,256]{1,0:T(8,128)(2,1)S(1)}, bf16[256,256]{1,0:T(8,128)(2,1)}, u32[]{:S(2)}) copy-start(bf16[256,256]{1,0:T(8,128)(2,1)} %param.24) | copy-start | bytes 393220
where the time goes:
time: 79.8 us; the launch traced here: 78.9 us
  blocking collectives  36.9 us (46%)
  starting transfers between devices  15.7 us (20%)
  matrix products  12.9 us (16%)
  other arithmetic  4.59 us (6%)
  waiting for transfers between devices  4.19 us (5%)
  local copies, waits for them, and re-layouts  2.96 us (4%)
  between operations  1.72 us (2%)
    all_gather x1, blocking collectives, body(): all_pointers = lax.all_gather(pointers, 'tm', axis=0, tiled=True)  32.6 us
    ppermute x3, starting transfers between devices, from_behind(): return lax.ppermute(block, axis, route)  11.4 us
    ppermute x3, waiting for transfers between devices, from_behind(): return lax.ppermute(block, axis, route)  4.18 us
    ppermute x1, starting transfers between devices, with_halo(): lax.ppermute(lax.slice_in_dim(block, block.shape[dim] - width, None, axis...  3.03 us
    psum x1, blocking collectives, body(): pooled = lax.psum(partial_value, 'space')  2.45 us
    all_gather x1, blocking collectives, body(): carried = lax.all_gather(memory, 'space', axis=1, tiled=True)  1.83 us
  transfers between devices with their start and end apart: 5, of which 1 were waited for; matrix products, arithmetic and copies ran while one was open for 15% of the time, Pallas kernels for 0%

commit v1 on v0

--- a/solution.py
+++ b/solution.py
@@ -1,10 +1,352 @@
+import functools
+
 import jax
 import jax.numpy as jnp
 from jax import lax
+from jax.experimental import pallas as pl
+from jax.experimental.pallas import tpu as pltpu
 from jax.sharding import PartitionSpec as P
 
 MEMS = 3
 POINTERS = 16
+MESH = pl.DeviceIdType.MESH
+F32 = jnp.float32
+BF16 = jnp.bfloat16
+
+
+def mm(a, b):
+    return jnp.dot(a, b, preferred_element_type=F32)
+
+
+def mm_t(a, b):
+    return lax.dot_general(a, b, (((1,), (1,)), ((), ())), preferred_element_type=F32)
+
+
+def kernel(
+    frames,
+    features,
+    masks,
+    mask_embed,
+    mem_tpos,
+    ptr_tpos,
+    empty_memory,
+    w_pix,
+    w_conv,
+    w_out_t,
+    w_ptr,
+    w_query,
+    w_key,
+    w_value,
+    w_proj,
+    attended,
+    memory,
+    pointers,
+    feat,
+    pix,
+    taps,
+    outw,
+    ptrw,
+    queryw,
+    key_pad,
+    value_pad,
+    projw,
+    joined,
+    halo,
+    conv,
+    part,
+    part_in,
+    mem_rows,
+    mem_send,
+    mem_in,
+    ptr_send,
+    ptr_in,
+    scores,
+    values,
+    load_sem,
+    near_send,
+    near_recv,
+    mem_send_sem,
+    mem_recv_sem,
+    ptr_send_sem,
+    ptr_recv_sem,
+):
+    _, rows, columns, dim = features.shape
+    tokens = rows * columns
+    mem_dim = w_key.shape[0]
+    half = tokens // 2
+    parts = dim // mem_dim
+    t = lax.axis_index("tm")
+    s = lax.axis_index("space")
+    other = 1 - s
+    reach = min(POINTERS, frames - 1)
+    mem_reach = min(MEMS, frames - 1)
+
+    barrier = pltpu.get_barrier_semaphore()
+    pl.semaphore_signal(barrier, inc=1, device_id=(t, other), device_id_type=MESH)
+    for d in range(reach, 0, -1):
+
+        @pl.when(t - d >= 0)
+        def _(d=d):
+            pl.semaphore_signal(barrier, inc=1, device_id=(t - d, s), device_id_type=MESH)
+            if d <= mem_reach:
+                pl.semaphore_signal(
+                    barrier, inc=1, device_id=(t - d, other), device_id_type=MESH
+                )
+
+    loads = []
+
+    def load(src, dst):
+        copy = pltpu.make_async_copy(src, dst, load_sem.at[len(loads)])
+        copy.start()
+        loads.append(copy)
+        return copy
+
+    feat_load = load(features.at[0], feat)
+    pix_load = load(w_pix, pix)
+    tap_loads = [load(w_conv.at[a], taps.at[a]) for a in range(3)]
+    query_load = load(w_query, queryw)
+    ptr_load = load(w_ptr, ptrw)
+    out_loads = [load(w_out_t, outw.at[pl.ds(k * mem_dim, mem_dim)]) for k in range(2)]
+    key_load = load(w_key, key_pad.at[pl.ds(mem_dim, mem_dim)])
+    value_load = load(w_value, value_pad.at[pl.ds(mem_dim, mem_dim)])
+    proj_load = load(w_proj, projw)
+
+    blank = jnp.zeros((mem_dim, dim), BF16)
+    for ref in (key_pad, value_pad):
+        ref[0:mem_dim] = blank
+        ref[2 * mem_dim : 3 * mem_dim] = blank
+    joined[0] = jnp.zeros((columns, dim), BF16)
+    joined[rows + 1] = jnp.zeros((columns, dim), BF16)
+    for d in range(1, MEMS + 1):
+
+        @pl.when(t - d < 0)
+        def _(d=d):
+            mem_in[d - 1] = jnp.zeros((2, half, 2 * mem_dim), BF16)
+
+    for d in range(1, POINTERS + 1):
+
+        @pl.when(t - d < 0)
+        def _(d=d):
+            ptr_in[d - 1] = jnp.zeros((1, dim), F32)
+
+    mask_f = masks[0].astype(F32)
+    spread = jnp.concatenate(
+        [jnp.broadcast_to(mask_f[r : r + 1], (columns, columns)) for r in range(rows)], axis=0
+    )
+    token_col = lax.broadcasted_iota(jnp.int32, (tokens, columns), 0) % columns
+    lane_col = lax.broadcasted_iota(jnp.int32, (tokens, columns), 1)
+    mask_col = jnp.sum(jnp.where(token_col == lane_col, spread, 0.0), axis=1, keepdims=True)
+    col_of = lax.broadcasted_iota(jnp.int32, (tokens, dim), 0) % columns
+
+    feat_load.wait()
+    flat = feat[...].reshape(tokens, dim)
+    flat_f = flat.astype(F32)
+    part[...] = jnp.sum(mask_col * flat_f, axis=0, keepdims=True)
+    pix_load.wait()
+    joined_rows = (
+        mm(flat, pix[...]) + mask_col * mask_embed[...].astype(F32).reshape(1, dim)
+    ).astype(BF16)
+    joined[1 : rows + 1] = joined_rows.reshape(rows, columns, dim)
+
+    sums = [None, None, None]
+    for a in range(3):
+        tap_loads[a].wait()
+        window = joined[a : a + rows].reshape(tokens, dim)
+        for b in range(3):
+            product = mm(window, taps[a, b])
+            sums[b] = product if sums[b] is None else sums[b] + product
+
+    def shift_columns(low, mid, high, col):
+        count = low.shape[0]
+        low = jnp.where(col == 0, 0.0, pltpu.roll(low, 1, 0))
+        high = jnp.where(col == columns - 1, 0.0, pltpu.roll(high, count - 1, 0))
+        return mid + low + high
+
+    conv[...] = shift_columns(*sums, col_of)
+
+    centred = flat_f - jnp.mean(flat_f, axis=1, keepdims=True)
+    query_in = (
+        centred * lax.rsqrt(jnp.mean(centred * centred, axis=1, keepdims=True) + 1e-05)
+    ).astype(BF16)
+    query_load.wait()
+    query = (mm(query_in, queryw[...]) * dim ** (-0.5)).astype(BF16)
+    ptr_load.wait()
+    for out_load in out_loads:
+        out_load.wait()
+
+    peers = 1
+    for d in range(1, reach + 1):
+        peers = peers + (1 - (t + d) // frames) * (2 if d <= mem_reach else 1)
+    pl.semaphore_wait(barrier, peers)
+
+    part_copy = pltpu.make_async_remote_copy(
+        src_ref=part,
+        dst_ref=part_in,
+        send_sem=near_send.at[0],
+        recv_sem=near_recv.at[0],
+        device_id=(t, other),
+        device_id_type=MESH,
+    )
+    part_copy.start()
+    halo_copy = pltpu.make_async_remote_copy(
+        src_ref=joined.at[1 + other * (rows - 1)],
+        dst_ref=halo,
+        send_sem=near_send.at[1],
+        recv_sem=near_recv.at[1],
+        device_id=(t, other),
+        device_id_type=MESH,
+    )
+    halo_copy.start()
+
+    key_load.wait()
+    value_load.wait()
+    key_w = key_pad[mem_dim : 2 * mem_dim]
+    value_w = value_pad[mem_dim : 2 * mem_dim]
+    mem_tpos_keys = mm(mem_tpos[...], key_w)
+
+    def cut(pointer_rows):
+        return jnp.concatenate(
+            [pointer_rows[:, j * mem_dim : (j + 1) * mem_dim] for j in range(parts)], axis=0
+        )
+
+    ptr_tokens = parts * POINTERS
+    ptr_tpos_keys = mm(cut(ptr_tpos[...]), key_w)
+    null_rows = jnp.broadcast_to(
+        empty_memory[...].astype(F32).reshape(1, mem_dim), (ptr_tokens, mem_dim)
+    ).astype(BF16)
+    null_keys = mm(null_rows, key_w).astype(BF16)
+    null_values = mm(null_rows, value_w).astype(BF16)
+
+    part_copy.wait()
+    pooled = part[...] + part_in[...]
+    pooled = jnp.broadcast_to(pooled, (8, dim))
+    normed = (
+        pooled * lax.rsqrt(jnp.mean(pooled * pooled, axis=1, keepdims=True) + 1e-06)
+    ).astype(BF16)
+    pointer = mm(normed, ptrw[...]).astype(BF16)[0:1]
+    ptr_send[0] = pointer.astype(F32)
+
+    def ptr_copy(d):
+        return pltpu.make_async_remote_copy(
+            src_ref=ptr_send.at[0],
+            dst_ref=ptr_in.at[d - 1],
+            send_sem=ptr_send_sem.at[d - 1],
+            recv_sem=ptr_recv_sem.at[d - 1],
+            device_id=(t + d, s),
+            device_id_type=MESH,
+        )
+
+    def mem_copy(d, to):
+        return pltpu.make_async_remote_copy(
+            src_ref=mem_send,
+            dst_ref=mem_in.at[d - 1, s],
+            send_sem=mem_send_sem.at[d - 1, to],
+            recv_sem=mem_recv_sem.at[d - 1, s],
+            device_id=(t + d, to),
+            device_id_type=MESH,
+        )
+
+    for d in range(reach, 0, -1):
+
+        @pl.when(t + d < frames)
+        def _(d=d):
+            ptr_copy(d).start()
+
+    pointers[...] = pointer
+
+    halo_copy.wait()
+    tap = 2 * other
+    edge = [mm(halo[...], taps[tap, b]) for b in range(3)]
+    edge_rows = pl.ds(other * (tokens - columns), columns)
+    conv[edge_rows] = conv[edge_rows] + shift_columns(*edge, col_of[0:columns])
+
+    v = conv[...]
+    hidden = (0.5 * v * (1.0 + jnp.tanh(0.7978845608 * (v + 0.044715 * (v * v * v))))).astype(BF16)
+    twice = mm_t(hidden, outw[...])
+    lane = lax.broadcasted_iota(jnp.int32, (half, 2 * mem_dim), 1)
+    mem_send[...] = jnp.where(lane < mem_dim, twice[0:half], twice[half:tokens]).astype(BF16)
+    for d in range(mem_reach, 0, -1):
+
+        @pl.when(t + d < frames)
+        def _(d=d):
+            for to in range(2):
+                mem_copy(d, to).start()
+
+    mem_rows[...] = twice
+    for c in range(0, columns, 2):
+        even = mem_rows[pl.ds(c, rows, stride=columns), :]
+        odd = mem_rows[pl.ds(c + 1, rows, stride=columns), :]
+        memory[0, :, c * mem_dim : (c + 2) * mem_dim] = jnp.where(
+            lane[0:rows] < mem_dim, even, odd
+        ).astype(BF16)
+
+    top = None
+    key_low, key_high = key_pad[mem_dim : 3 * mem_dim], key_pad[0 : 2 * mem_dim]
+    value_low, value_high = value_pad[mem_dim : 3 * mem_dim], value_pad[0 : 2 * mem_dim]
+    column = 0
+
+    def put(keys, vals, valid, at, top):
+        count = keys.shape[0]
+        block = jnp.where(valid, mm_t(query, keys), -jnp.inf)
+        scores[:, at : at + count] = block
+        values[at : at + count] = vals
+        peak = jnp.max(block, axis=1, keepdims=True)
+        return peak if top is None else jnp.maximum(top, peak)
+
+    for d in range(1, MEMS + 1):
+        for band in range(2):
+
+            @pl.when(t - d >= 0)
+            def _(d=d, band=band):
+                pltpu.make_async_remote_copy(
+                    src_ref=mem_send,
+                    dst_ref=mem_in.at[d - 1, band],
+                    send_sem=mem_send_sem.at[d - 1, band],
+                    recv_sem=mem_recv_sem.at[d - 1, band],
+                    device_id=(t, other),
+                    device_id_type=MESH,
+                ).wait_recv()
+
+        packed = mem_in[d - 1].reshape(tokens, 2 * mem_dim)
+        tpos = mem_tpos_keys[d - 1 : d]
+        for key_half, value_half in ((key_low, value_low), (key_high, value_high)):
+            keys = (mm(packed, key_half) + tpos).astype(BF16)
+            vals = mm(packed, value_half).astype(BF16)
+            top = put(keys, vals, t - d >= 0, column, top)
+            column += tokens
+
+    for d in range(1, reach + 1):
+
+        @pl.when(t - d >= 0)
+        def _(d=d):
+            ptr_copy(d).wait_recv()
+
+    tokens_in = cut(ptr_in[...].reshape(POINTERS, dim).astype(BF16))
+    keys = jnp.concatenate(
+        [(mm(tokens_in, key_w) + ptr_tpos_keys).astype(BF16), null_keys], axis=0
+    )
+    vals = jnp.concatenate([mm(tokens_in, value_w).astype(BF16), null_values], axis=0)
+    index = lax.broadcasted_iota(jnp.int32, (1, 2 * ptr_tokens), 1)
+    oldest = t - 1 - index % POINTERS
+    valid = ((index < ptr_tokens) & (oldest >= 0)) | (index == ptr_tokens)
+    top = put(keys, vals, valid, column, top)
+
+    weights = jnp.exp(scores[...] - top)
+    total = jnp.sum(weights, axis=1, keepdims=True)
+    weights = (weights * (1.0 / total)).astype(BF16)
+    mixed = mm(weights, values[...]).astype(BF16)
+    proj_load.wait()
+    result = feat[...].reshape(tokens, dim).astype(F32) + mm(mixed, projw[...])
+    attended[0] = result.astype(BF16).reshape(rows, columns, dim)
+
+    for d in range(1, reach + 1):
+
+        @pl.when(t + d < frames)
+        def _(d=d):
+            ptr_copy(d).wait_send()
+            if d <= mem_reach:
+                for to in range(2):
+                    mem_copy(d, to).wait_send()
 
 
 def from_behind(block, axis, distance):
@@ -54,7 +396,7 @@
     return mixed_sum.astype(jnp.bfloat16)
 
 
-def body(
+def staged_body(
     features,
     masks,
     w_pix,
@@ -181,26 +523,103 @@
     return (attended, memory, pointers)
 
 
+def fused_body(
+    features,
+    masks,
+    w_pix,
+    mask_embed,
+    w_conv,
+    w_out,
+    w_ptr,
+    w_query,
+    w_key,
+    w_value,
+    w_proj,
+    mem_tpos,
+    ptr_tpos,
+    empty_memory,
+):
+    _, rows, columns, dim = features.shape
+    frames = lax.axis_size("tm")
+    mem_dim = w_key.shape[0]
+    tokens = rows * columns
+    half = tokens // 2
+    key_count = MEMS * 2 * tokens + 2 * POINTERS * (dim // mem_dim)
+    vmem = pl.BlockSpec(memory_space=pltpu.VMEM)
+    hbm = pl.BlockSpec(memory_space=pl.ANY)
+    dma = pltpu.SemaphoreType.DMA
+    return pl.pallas_call(
+        functools.partial(kernel, frames),
+        out_shape=(
+            jax.ShapeDtypeStruct(features.shape, BF16),
+            jax.ShapeDtypeStruct((1, rows, columns * mem_dim), BF16),
+            jax.ShapeDtypeStruct((1, dim), BF16),
+        ),
+        in_specs=[hbm] + [vmem] * 5 + [hbm] * 8,
+        out_specs=(vmem, vmem, vmem),
+        scratch_shapes=[
+            pltpu.VMEM((rows, columns, dim), BF16),
+            pltpu.VMEM(w_pix.shape, BF16),
+            pltpu.VMEM(w_conv.shape, BF16),
+            pltpu.VMEM((2 * mem_dim, dim), BF16),
+            pltpu.VMEM(w_ptr.shape, BF16),
+            pltpu.VMEM(w_query.shape, BF16),
+            pltpu.VMEM((3 * mem_dim, dim), BF16),
+            pltpu.VMEM((3 * mem_dim, dim), BF16),
+            pltpu.VMEM(w_proj.shape, BF16),
+            pltpu.VMEM((rows + 2, columns, dim), BF16),
+            pltpu.VMEM((columns, dim), BF16),
+            pltpu.VMEM((tokens, dim), F32),
+            pltpu.VMEM((1, dim), F32),
+            pltpu.VMEM((1, dim), F32),
+            pltpu.VMEM((tokens, 2 * mem_dim), F32),
+            pltpu.VMEM((half, 2 * mem_dim), BF16),
+            pltpu.VMEM((MEMS, 2, half, 2 * mem_dim), BF16),
+            pltpu.VMEM((1, 1, dim), F32),
+            pltpu.VMEM((POINTERS, 1, dim), F32),
+            pltpu.VMEM((tokens, key_count), F32),
+            pltpu.VMEM((key_count, dim), BF16),
+            dma((12,)),
+            dma((2,)),
+            dma((2,)),
+            dma((MEMS, 2)),
+            dma((MEMS, 2)),
+            dma((POINTERS,)),
+            dma((POINTERS,)),
+        ],
+        compiler_params=pltpu.CompilerParams(collective_id=0, has_side_effects=True),
+    )(
+        features,
+        masks,
+        mask_embed,
+        mem_tpos,
+        ptr_tpos,
+        empty_memory,
+        w_pix,
+        w_conv,
+        w_out.T,
+        w_ptr,
+        w_query,
+        w_key,
+        w_value,
+        w_proj,
+    )
+
+
+def body(features, *rest):
+    frames_dev, rows, columns, dim = features.shape
+    key_count = MEMS * 2 * rows * columns
+    fits = rows * columns * key_count * 4 <= 2**23 and rows * columns <= 256
+    if frames_dev == 1 and lax.axis_size("space") == 2 and fits:
+        return fused_body(features, *rest)
+    return staged_body(features, *rest)
+
+
 def solution(mesh):
     return jax.shard_map(
         body,
         mesh=mesh,
-        in_specs=(
-            P("tm", "space", None, None),
-            P("tm", "space", None),
-            P(),
-            P(),
-            P(),
-            P(),
-            P(),
-            P(),
-            P(),
-            P(),
-            P(),
-            P(),
-            P(),
-            P(),
-        ),
+        in_specs=(P("tm", "space", None, None), P("tm", "space", None)) + (P(),) * 12,
         out_specs=(P("tm", "space", None, None), P("tm", "space", None), P("tm", None)),
         check_vma=False,
     )

time: 79.8 us -> 20.1 us (0.25)
  the two profiles are of different devices: /device:TPU:24 before, /device:TPU:9 now
where the time goes in v1:
time: 20.1 us; the launch traced here: 19.8 us
  Pallas kernels  15.2 us (76%)
  local copies, waits for them, and re-layouts  4.02 us (20%)
  between operations  0.65 us (3%)
    pallas_call x1, Pallas kernels, fused_body(): pl.pallas_call(functools.partial(kernel, frames), out_shape=(jax.ShapeDty...  15.2 us
    unnamed x3, local copies, waits for them, and re-layouts  4.02 us

profile of v1, /device:TPU:9, one launch (start us, length us, event | category | flops | bytes accessed | tf_op | source)
XLA Modules:
  0.0 19.8 jit_solution(17262738658787480992)
XLA Ops:
  0.6 15.2 %shard_map.157 = (bf16[1,8,16,256]{3,2,1,0:T(8,128)(2,1)}, bf16[1,8,1024]{2,1,0:T(8,128)(2,1)}, bf16[1,256]{1,0:T(2,128)(2,1)}) custom-call(bf16[1,8,16,256]{3,2,1,0:T(8,128)(2,1)} %features.1, s32[1,8,16]{2,1,0:T(8,128)} %masks.1, bf16[256]{0:T(256)(128)(2,1)} %mask_embed.1, bf16[3,64]{1,0:T(4,128)(2,1)} %mem_tpos.1, bf16[16,256]{1,0:T(8,128)(2,1)} %ptr_tpos.1, ...), custom_call_target="tpu_custom_call" | custom-call | tf_op jit(solution)/shard_map/pallas_call | solution.py:551
  15.8 1.5 %copy.20 = bf16[1,8,16,256]{3,2,1,0:T(8,128)(2,1)} copy(bf16[1,8,16,256]{3,2,1,0:T(8,128)(2,1)} %get-tuple-element.6) | data formatting | bytes 131072
  17.3 1.3 %copy.21 = bf16[1,8,1024]{2,1,0:T(8,128)(2,1)} copy(bf16[1,8,1024]{2,1,0:T(8,128)(2,1)} %get-tuple-element.7) | data formatting | bytes 32768
  18.6 1.2 %copy.22 = bf16[1,256]{1,0:T(2,128)(2,1)} copy(bf16[1,256]{1,0:T(2,128)(2,1)} %get-tuple-element.8) | data formatting | bytes 1024

commit v2 on v1

--- a/solution.py
+++ b/solution.py
@@ -25,11 +25,11 @@
 def kernel(
     frames,
     features,
-    masks,
-    mask_embed,
-    mem_tpos,
-    ptr_tpos,
-    empty_memory,
+    masks_in,
+    mask_embed_in,
+    mem_tpos_in,
+    ptr_tpos_in,
+    empty_memory_in,
     w_pix,
     w_conv,
     w_out_t,
@@ -42,6 +42,11 @@
     memory,
     pointers,
     feat,
+    masks,
+    mask_embed,
+    mem_tpos,
+    ptr_tpos,
+    empty_memory,
     pix,
     taps,
     outw,
@@ -102,6 +107,8 @@
         return copy
 
     feat_load = load(features.at[0], feat)
+    mask_load = load(masks_in, masks)
+    embed_load = load(mask_embed_in, mask_embed)
     pix_load = load(w_pix, pix)
     tap_loads = [load(w_conv.at[a], taps.at[a]) for a in range(3)]
     query_load = load(w_query, queryw)
@@ -109,6 +116,11 @@
     out_loads = [load(w_out_t, outw.at[pl.ds(k * mem_dim, mem_dim)]) for k in range(2)]
     key_load = load(w_key, key_pad.at[pl.ds(mem_dim, mem_dim)])
     value_load = load(w_value, value_pad.at[pl.ds(mem_dim, mem_dim)])
+    small_loads = [
+        load(mem_tpos_in, mem_tpos),
+        load(ptr_tpos_in, ptr_tpos),
+        load(empty_memory_in, empty_memory),
+    ]
     proj_load = load(w_proj, projw)
 
     blank = jnp.zeros((mem_dim, dim), BF16)
@@ -129,6 +141,7 @@
         def _(d=d):
             ptr_in[d - 1] = jnp.zeros((1, dim), F32)
 
+    mask_load.wait()
     mask_f = masks[0].astype(F32)
     spread = jnp.concatenate(
         [jnp.broadcast_to(mask_f[r : r + 1], (columns, columns)) for r in range(rows)], axis=0
@@ -143,6 +156,7 @@
     flat_f = flat.astype(F32)
     part[...] = jnp.sum(mask_col * flat_f, axis=0, keepdims=True)
     pix_load.wait()
+    embed_load.wait()
     joined_rows = (
         mm(flat, pix[...]) + mask_col * mask_embed[...].astype(F32).reshape(1, dim)
     ).astype(BF16)
@@ -200,6 +214,8 @@
 
     key_load.wait()
     value_load.wait()
+    for small_load in small_loads:
+        small_load.wait()
     key_w = key_pad[mem_dim : 2 * mem_dim]
     value_w = value_pad[mem_dim : 2 * mem_dim]
     mem_tpos_keys = mm(mem_tpos[...], key_w)
@@ -523,6 +539,15 @@
     return (attended, memory, pointers)
 
 
+def put_out(*refs):
+    sem = refs[-1]
+    copies = [pltpu.make_async_copy(refs[k], refs[3 + k], sem.at[k]) for k in range(3)]
+    for copy in copies:
+        copy.start()
+    for copy in copies:
+        copy.wait()
+
+
 def fused_body(
     features,
     masks,
@@ -546,19 +571,24 @@
     half = tokens // 2
     key_count = MEMS * 2 * tokens + 2 * POINTERS * (dim // mem_dim)
     vmem = pl.BlockSpec(memory_space=pltpu.VMEM)
-    hbm = pl.BlockSpec(memory_space=pl.ANY)
+    hbm = pl.BlockSpec(memory_space=pltpu.HBM)
     dma = pltpu.SemaphoreType.DMA
-    return pl.pallas_call(
+    results = pl.pallas_call(
         functools.partial(kernel, frames),
         out_shape=(
-            jax.ShapeDtypeStruct(features.shape, BF16),
-            jax.ShapeDtypeStruct((1, rows, columns * mem_dim), BF16),
-            jax.ShapeDtypeStruct((1, dim), BF16),
+            pltpu.VMEM(features.shape, BF16),
+            pltpu.VMEM((1, rows, columns * mem_dim), BF16),
+            pltpu.VMEM((1, dim), BF16),
         ),
-        in_specs=[hbm] + [vmem] * 5 + [hbm] * 8,
+        in_specs=[hbm] * 14,
         out_specs=(vmem, vmem, vmem),
         scratch_shapes=[
             pltpu.VMEM((rows, columns, dim), BF16),
+            pltpu.VMEM(masks.shape, masks.dtype),
+            pltpu.VMEM(mask_embed.shape, BF16),
+            pltpu.VMEM(mem_tpos.shape, BF16),
+            pltpu.VMEM(ptr_tpos.shape, BF16),
+            pltpu.VMEM(empty_memory.shape, BF16),
             pltpu.VMEM(w_pix.shape, BF16),
             pltpu.VMEM(w_conv.shape, BF16),
             pltpu.VMEM((2 * mem_dim, dim), BF16),
@@ -579,7 +609,7 @@
             pltpu.VMEM((POINTERS, 1, dim), F32),
             pltpu.VMEM((tokens, key_count), F32),
             pltpu.VMEM((key_count, dim), BF16),
-            dma((12,)),
+            dma((17,)),
             dma((2,)),
             dma((2,)),
             dma((MEMS, 2)),
@@ -587,7 +617,9 @@
             dma((POINTERS,)),
             dma((POINTERS,)),
         ],
-        compiler_params=pltpu.CompilerParams(collective_id=0, has_side_effects=True),
+        compiler_params=pltpu.CompilerParams(
+            collective_id=0, has_side_effects=True
+        ),
     )(
         features,
         masks,
@@ -604,6 +636,14 @@
         w_value,
         w_proj,
     )
+    return pl.pallas_call(
+        put_out,
+        out_shape=tuple(jax.ShapeDtypeStruct(x.shape, x.dtype) for x in results),
+        in_specs=[vmem] * 3,
+        out_specs=(hbm,) * 3,
+        scratch_shapes=[dma((3,))],
+        compiler_params=pltpu.CompilerParams(vmem_limit_bytes=2**20),
+    )(*[pltpu.with_memory_space_constraint(x, pltpu.VMEM) for x in results])
 
 
 def body(features, *rest):

time: 20.1 us -> 15.3 us (0.76)
  local copies, waits for them, and re-layouts: 4.02 us -> 0 us
  Pallas kernels: 15.2 us -> 14.5 us
    unnamed x3 -> x0, local copies, waits for them, and re-layouts: 4.02 us -> none
    pallas_call x1 -> x2, Pallas kernels: 15.2 us -> 14.5 us  [the longest x1 13.9 us: fused_body(): pl.pallas_call(functools.partial(kernel, frames), out_shape=(pltpu.VMEM(f...]
where the time goes in v2:
time: 15.3 us; the launch traced here: 15.2 us
  Pallas kernels  14.5 us (95%)
  between operations  0.64 us (4%)
    pallas_call x1, Pallas kernels, fused_body(): pl.pallas_call(functools.partial(kernel, frames), out_shape=(pltpu.VMEM(f...  13.9 us
    pallas_call x1, Pallas kernels, fused_body(): pl.pallas_call(put_out, out_shape=tuple((jax.ShapeDtypeStruct(x.shape, x....  0.66 us

profile of v2, /device:TPU:9, one launch (start us, length us, event | category | flops | bytes accessed | tf_op | source)
XLA Modules:
  0.0 15.2 jit_solution(8502242199768464044)
XLA Ops:
  0.6 13.9 %shard_map.157 = (bf16[1,8,16,256]{3,2,1,0:T(8,128)(2,1)S(1)}, bf16[1,8,1024]{2,1,0:T(8,128)(2,1)S(1)}, bf16[1,256]{1,0:T(2,128)(2,1)S(1)}) custom-call(bf16[1,8,16,256]{3,2,1,0:T(8,128)(2,1)} %features.1, s32[1,8,16]{2,1,0:T(8,128)} %masks_in.1, bf16[256]{0:T(256)(128)(2,1)} %mask_embed_in.1, bf16[3,64]{1,0:T(4,128)(2,1)} %mem_tpos_in.1, ...), custom_call_target="tpu_custom_call" | custom-call | tf_op jit(solution)/shard_map/pallas_call | solution.py:576
  14.5 0.7 %shard_map.158 = (bf16[1,8,16,256]{3,2,1,0:T(8,128)(2,1)}, bf16[1,8,1024]{2,1,0:T(8,128)(2,1)}, bf16[1,256]{1,0:T(2,128)(2,1)}) custom-call(bf16[1,8,16,256]{3,2,1,0:T(8,128)(2,1)S(1)} %get-tuple-element.6.refs_0_, bf16[1,8,1024]{2,1,0:T(8,128)(2,1)S(1)} %get-tuple-element.7.refs_1_, bf16[1,256]{1,0:T(2,128)(2,1)S(1)} %get-tuple-element.8.refs_2_), custom_call_target="tpu_custom_call" | custom-call | tf_op jit(solution)/shard_map/pallas_call | solution.py:639

commit v3 on v2

--- a/solution.py
+++ b/solution.py
@@ -9,6 +9,7 @@
 
 MEMS = 3
 POINTERS = 16
+BLOCK_ORDER = (1, 2, 0, 3)
 MESH = pl.DeviceIdType.MESH
 F32 = jnp.float32
 BF16 = jnp.bfloat16
@@ -59,21 +60,21 @@
     halo,
     conv,
     part,
-    part_in,
+    part_near,
+    parts_in,
     mem_rows,
     mem_send,
+    edge_send,
     mem_in,
-    ptr_send,
-    ptr_in,
-    scores,
-    values,
     load_sem,
     near_send,
     near_recv,
     mem_send_sem,
     mem_recv_sem,
-    ptr_send_sem,
-    ptr_recv_sem,
+    edge_send_sem,
+    edge_recv_sem,
+    part_send_sem,
+    part_recv_sem,
 ):
     _, rows, columns, dim = features.shape
     tokens = rows * columns
@@ -85,18 +86,6 @@
     other = 1 - s
     reach = min(POINTERS, frames - 1)
     mem_reach = min(MEMS, frames - 1)
-
-    barrier = pltpu.get_barrier_semaphore()
-    pl.semaphore_signal(barrier, inc=1, device_id=(t, other), device_id_type=MESH)
-    for d in range(reach, 0, -1):
-
-        @pl.when(t - d >= 0)
-        def _(d=d):
-            pl.semaphore_signal(barrier, inc=1, device_id=(t - d, s), device_id_type=MESH)
-            if d <= mem_reach:
-                pl.semaphore_signal(
-                    barrier, inc=1, device_id=(t - d, other), device_id_type=MESH
-                )
 
     loads = []
 
@@ -123,6 +112,16 @@
     ]
     proj_load = load(w_proj, projw)
 
+    barrier = pltpu.get_barrier_semaphore()
+    for d in range(reach, 0, -1):
+
+        @pl.when(t - d >= 0)
+        def _(d=d):
+            for to in range(2):
+                pl.semaphore_signal(barrier, inc=1, device_id=(t - d, to), device_id_type=MESH)
+
+    pl.semaphore_signal(barrier, inc=1, device_id=(t, other), device_id_type=MESH)
+
     blank = jnp.zeros((mem_dim, dim), BF16)
     for ref in (key_pad, value_pad):
         ref[0:mem_dim] = blank
@@ -139,7 +138,7 @@
 
         @pl.when(t - d < 0)
         def _(d=d):
-            ptr_in[d - 1] = jnp.zeros((1, dim), F32)
+            parts_in[d - 1] = jnp.zeros((2, 1, dim), F32)
 
     mask_load.wait()
     mask_f = masks[0].astype(F32)
@@ -176,7 +175,18 @@
         high = jnp.where(col == columns - 1, 0.0, pltpu.roll(high, count - 1, 0))
         return mid + low + high
 
-    conv[...] = shift_columns(*sums, col_of)
+    def encode(v):
+        gelu = 0.5 * v * (1.0 + jnp.tanh(0.7978845608 * (v + 0.044715 * (v * v * v))))
+        return mm_t(gelu.astype(BF16), outw[...])
+
+    conv_sum = shift_columns(*sums, col_of)
+    conv[...] = conv_sum
+    for out_load in out_loads:
+        out_load.wait()
+    twice = encode(conv_sum)
+    lane = lax.broadcasted_iota(jnp.int32, (half, 2 * mem_dim), 1)
+    mem_rows[...] = twice
+    mem_send[...] = jnp.where(lane < mem_dim, twice[0:half], twice[half:tokens]).astype(BF16)
 
     centred = flat_f - jnp.mean(flat_f, axis=1, keepdims=True)
     query_in = (
@@ -185,32 +195,77 @@
     query_load.wait()
     query = (mm(query_in, queryw[...]) * dim ** (-0.5)).astype(BF16)
     ptr_load.wait()
-    for out_load in out_loads:
-        out_load.wait()
-
     peers = 1
     for d in range(1, reach + 1):
-        peers = peers + (1 - (t + d) // frames) * (2 if d <= mem_reach else 1)
+        peers = peers + (1 - (t + d) // frames) * 2
     pl.semaphore_wait(barrier, peers)
 
-    part_copy = pltpu.make_async_remote_copy(
-        src_ref=part,
-        dst_ref=part_in,
-        send_sem=near_send.at[0],
-        recv_sem=near_recv.at[0],
-        device_id=(t, other),
-        device_id_type=MESH,
-    )
-    part_copy.start()
-    halo_copy = pltpu.make_async_remote_copy(
-        src_ref=joined.at[1 + other * (rows - 1)],
-        dst_ref=halo,
-        send_sem=near_send.at[1],
-        recv_sem=near_recv.at[1],
-        device_id=(t, other),
-        device_id_type=MESH,
+    def send(src, dst, send_sem, recv_sem, frame, to):
+        return pltpu.make_async_remote_copy(
+            src_ref=src,
+            dst_ref=dst,
+            send_sem=send_sem,
+            recv_sem=recv_sem,
+            device_id=(frame, to),
+            device_id_type=MESH,
+        )
+
+    def part_copy(d, band, to):
+        return send(
+            part,
+            parts_in.at[d - 1, band],
+            part_send_sem.at[d - 1, to],
+            part_recv_sem.at[d - 1, band],
+            t + d,
+            to,
+        )
+
+    main = half - columns
+
+    def main_copy(d, band, to):
+        at = pl.ds(pl.multiple_of(band * columns, columns), main)
+        return send(
+            mem_send.at[at],
+            mem_in.at[d - 1, band, at],
+            mem_send_sem.at[d - 1, to],
+            mem_recv_sem.at[d - 1, band],
+            t + d,
+            to,
+        )
+
+    def edge_copy(d, band, to):
+        at = pl.ds(pl.multiple_of((1 - band) * main, columns), columns)
+        return send(
+            edge_send,
+            mem_in.at[d - 1, band, at],
+            edge_send_sem.at[d - 1, to],
+            edge_recv_sem.at[d - 1, band],
+            t + d,
+            to,
+        )
+
+    edge_at = pl.multiple_of(other * (tokens - columns), columns)
+    edge_rows = pl.ds(edge_at, columns)
+    halo_copy = send(
+        joined.at[1 + other * (rows - 1)], halo, near_send.at[1], near_recv.at[1], t, other
     )
     halo_copy.start()
+    for d in range(reach, 0, -1):
+
+        @pl.when(t + d < frames)
+        def _(d=d):
+            for to in range(2):
+                part_copy(d, s, to).start()
+
+    for d in range(mem_reach, 0, -1):
+
+        @pl.when(t + d < frames)
+        def _(d=d):
+            for to in range(2):
+                main_copy(d, s, to).start()
+
+    near_copy = send(part, part_near, near_send.at[0], near_recv.at[0], t, other)
+    near_copy.start()
 
     key_load.wait()
     value_load.wait()
@@ -233,62 +288,21 @@
     null_keys = mm(null_rows, key_w).astype(BF16)
     null_values = mm(null_rows, value_w).astype(BF16)
 
-    part_copy.wait()
-    pooled = part[...] + part_in[...]
-    pooled = jnp.broadcast_to(pooled, (8, dim))
-    normed = (
-        pooled * lax.rsqrt(jnp.mean(pooled * pooled, axis=1, keepdims=True) + 1e-06)
-    ).astype(BF16)
-    pointer = mm(normed, ptrw[...]).astype(BF16)[0:1]
-    ptr_send[0] = pointer.astype(F32)
-
-    def ptr_copy(d):
-        return pltpu.make_async_remote_copy(
-            src_ref=ptr_send.at[0],
-            dst_ref=ptr_in.at[d - 1],
-            send_sem=ptr_send_sem.at[d - 1],
-            recv_sem=ptr_recv_sem.at[d - 1],
-            device_id=(t + d, s),
-            device_id_type=MESH,
-        )
-
-    def mem_copy(d, to):
-        return pltpu.make_async_remote_copy(
-            src_ref=mem_send,
-            dst_ref=mem_in.at[d - 1, s],
-            send_sem=mem_send_sem.at[d - 1, to],
-            recv_sem=mem_recv_sem.at[d - 1, s],
-            device_id=(t + d, to),
-            device_id_type=MESH,
-        )
-
-    for d in range(reach, 0, -1):
-
-        @pl.when(t + d < frames)
-        def _(d=d):
-            ptr_copy(d).start()
-
-    pointers[...] = pointer
-
     halo_copy.wait()
     tap = 2 * other
     edge = [mm(halo[...], taps[tap, b]) for b in range(3)]
-    edge_rows = pl.ds(other * (tokens - columns), columns)
-    conv[edge_rows] = conv[edge_rows] + shift_columns(*edge, col_of[0:columns])
-
-    v = conv[...]
-    hidden = (0.5 * v * (1.0 + jnp.tanh(0.7978845608 * (v + 0.044715 * (v * v * v))))).astype(BF16)
-    twice = mm_t(hidden, outw[...])
-    lane = lax.broadcasted_iota(jnp.int32, (half, 2 * mem_dim), 1)
-    mem_send[...] = jnp.where(lane < mem_dim, twice[0:half], twice[half:tokens]).astype(BF16)
+    edge_twice = encode(conv[edge_rows] + shift_columns(*edge, col_of[0:columns]))
+    slab = mem_send[pl.ds(pl.multiple_of(other * main, columns), columns)].astype(F32)
+    side = (lane[0:columns] // mem_dim) == other
+    edge_send[...] = jnp.where(side, edge_twice, slab).astype(BF16)
     for d in range(mem_reach, 0, -1):
 
         @pl.when(t + d < frames)
         def _(d=d):
             for to in range(2):
-                mem_copy(d, to).start()
-
-    mem_rows[...] = twice
+                edge_copy(d, s, to).start()
+
+    mem_rows[edge_rows] = edge_twice
     for c in range(0, columns, 2):
         even = mem_rows[pl.ds(c, rows, stride=columns), :]
         odd = mem_rows[pl.ds(c + 1, rows, stride=columns), :]
@@ -296,61 +310,59 @@
             lane[0:rows] < mem_dim, even, odd
         ).astype(BF16)
 
-    top = None
+    def to_pointers(pooled):
+        normed = pooled * lax.rsqrt(jnp.mean(pooled * pooled, axis=1, keepdims=True) + 1e-06)
+        return mm(normed.astype(BF16), ptrw[...]).astype(BF16)
+
+    near_copy.wait()
+    pointers[...] = to_pointers(jnp.broadcast_to(part[...] + part_near[...], (8, dim)))[0:1]
+
     key_low, key_high = key_pad[mem_dim : 3 * mem_dim], key_pad[0 : 2 * mem_dim]
     value_low, value_high = value_pad[mem_dim : 3 * mem_dim], value_pad[0 : 2 * mem_dim]
-    column = 0
-
-    def put(keys, vals, valid, at, top):
-        count = keys.shape[0]
-        block = jnp.where(valid, mm_t(query, keys), -jnp.inf)
-        scores[:, at : at + count] = block
-        values[at : at + count] = vals
-        peak = jnp.max(block, axis=1, keepdims=True)
-        return peak if top is None else jnp.maximum(top, peak)
-
-    for d in range(1, MEMS + 1):
-        for band in range(2):
-
-            @pl.when(t - d >= 0)
-            def _(d=d, band=band):
-                pltpu.make_async_remote_copy(
-                    src_ref=mem_send,
-                    dst_ref=mem_in.at[d - 1, band],
-                    send_sem=mem_send_sem.at[d - 1, band],
-                    recv_sem=mem_recv_sem.at[d - 1, band],
-                    device_id=(t, other),
-                    device_id_type=MESH,
-                ).wait_recv()
+
+    def block(keys, vals, valid):
+        found = jnp.where(valid, mm_t(query, keys), -1e30)
+        top = jnp.max(found, axis=1, keepdims=True)
+        grown = jnp.exp(found - top)
+        return top, jnp.sum(grown, axis=1, keepdims=True), mm(grown.astype(BF16), vals)
+
+    def memory_block(d):
+        @pl.when(t - d >= 0)
+        def _():
+            for band in range(2):
+                main_copy(d, band, other).wait_recv()
+                edge_copy(d, band, other).wait_recv()
 
         packed = mem_in[d - 1].reshape(tokens, 2 * mem_dim)
         tpos = mem_tpos_keys[d - 1 : d]
-        for key_half, value_half in ((key_low, value_low), (key_high, value_high)):
-            keys = (mm(packed, key_half) + tpos).astype(BF16)
-            vals = mm(packed, value_half).astype(BF16)
-            top = put(keys, vals, t - d >= 0, column, top)
-            column += tokens
-
-    for d in range(1, reach + 1):
-
-        @pl.when(t - d >= 0)
-        def _(d=d):
-            ptr_copy(d).wait_recv()
-
-    tokens_in = cut(ptr_in[...].reshape(POINTERS, dim).astype(BF16))
-    keys = jnp.concatenate(
-        [(mm(tokens_in, key_w) + ptr_tpos_keys).astype(BF16), null_keys], axis=0
-    )
-    vals = jnp.concatenate([mm(tokens_in, value_w).astype(BF16), null_values], axis=0)
-    index = lax.broadcasted_iota(jnp.int32, (1, 2 * ptr_tokens), 1)
-    oldest = t - 1 - index % POINTERS
-    valid = ((index < ptr_tokens) & (oldest >= 0)) | (index == ptr_tokens)
-    top = put(keys, vals, valid, column, top)
-
-    weights = jnp.exp(scores[...] - top)
-    total = jnp.sum(weights, axis=1, keepdims=True)
-    weights = (weights * (1.0 / total)).astype(BF16)
-    mixed = mm(weights, values[...]).astype(BF16)
+        keys = [(mm(packed, w) + tpos).astype(BF16) for w in (key_low, key_high)]
+        vals = [mm(packed, w).astype(BF16) for w in (value_low, value_high)]
+        return block(jnp.concatenate(keys, axis=0), jnp.concatenate(vals, axis=0), t - d >= 0)
+
+    def pointer_block():
+        for d in range(1, reach + 1):
+
+            @pl.when(t - d >= 0)
+            def _(d=d):
+                for band in range(2):
+                    part_copy(d, band, other).wait_recv()
+
+        tokens_in = cut(to_pointers((parts_in[:, 0] + parts_in[:, 1]).reshape(POINTERS, dim)))
+        keys = jnp.concatenate(
+            [(mm(tokens_in, key_w) + ptr_tpos_keys).astype(BF16), null_keys], axis=0
+        )
+        vals = jnp.concatenate([mm(tokens_in, value_w).astype(BF16), null_values], axis=0)
+        index = lax.broadcasted_iota(jnp.int32, (1, 2 * ptr_tokens), 1)
+        oldest = t - 1 - index % POINTERS
+        valid = ((index < ptr_tokens) & (oldest >= 0)) | (index == ptr_tokens)
+        return block(keys, vals, valid)
+
+    blocks = [pointer_block() if d == 0 else memory_block(d) for d in BLOCK_ORDER]
+    top = functools.reduce(jnp.maximum, [b[0] for b in blocks])
+    factors = [jnp.exp(b[0] - top) for b in blocks]
+    total = sum(f * b[1] for f, b in zip(factors, blocks))
+    scale = 1.0 / total
+    mixed = sum((f * scale) * b[2] for f, b in zip(factors, blocks)).astype(BF16)
     proj_load.wait()
     result = feat[...].reshape(tokens, dim).astype(F32) + mm(mixed, projw[...])
     attended[0] = result.astype(BF16).reshape(rows, columns, dim)
@@ -359,10 +371,11 @@
 
         @pl.when(t + d < frames)
         def _(d=d):
-            ptr_copy(d).wait_send()
-            if d <= mem_reach:
-                for to in range(2):
-                    mem_copy(d, to).wait_send()
+            for to in range(2):
+                part_copy(d, s, to).wait_send()
+                if d <= mem_reach:
+                    main_copy(d, s, to).wait_send()
+                    edge_copy(d, s, to).wait_send()
 
 
 def from_behind(block, axis, distance):
@@ -569,7 +582,6 @@
     mem_dim = w_key.shape[0]
     tokens = rows * columns
     half = tokens // 2
-    key_count = MEMS * 2 * tokens + 2 * POINTERS * (dim // mem_dim)
     vmem = pl.BlockSpec(memory_space=pltpu.VMEM)
     hbm = pl.BlockSpec(memory_space=pltpu.HBM)
     dma = pltpu.SemaphoreType.DMA
@@ -602,20 +614,20 @@
             pltpu.VMEM((tokens, dim), F32),
             pltpu.VMEM((1, dim), F32),
             pltpu.VMEM((1, dim), F32),
+            pltpu.VMEM((POINTERS, 2, 1, dim), F32),
             pltpu.VMEM((tokens, 2 * mem_dim), F32),
             pltpu.VMEM((half, 2 * mem_dim), BF16),
+            pltpu.VMEM((columns, 2 * mem_dim), BF16),
             pltpu.VMEM((MEMS, 2, half, 2 * mem_dim), BF16),
-            pltpu.VMEM((1, 1, dim), F32),
-            pltpu.VMEM((POINTERS, 1, dim), F32),
-            pltpu.VMEM((tokens, key_count), F32),
-            pltpu.VMEM((key_count, dim), BF16),
             dma((17,)),
             dma((2,)),
             dma((2,)),
             dma((MEMS, 2)),
             dma((MEMS, 2)),
-            dma((POINTERS,)),
-            dma((POINTERS,)),
+            dma((MEMS, 2)),
+            dma((MEMS, 2)),
+            dma((POINTERS, 2)),
+            dma((POINTERS, 2)),
         ],
         compiler_params=pltpu.CompilerParams(
             collective_id=0, has_side_effects=True

time: 15.3 us -> 15.1 us (0.987)
  Pallas kernels: 14.5 us -> 14.3 us
    pallas_call x1, Pallas kernels: 13.9 us -> 13.6 us  [fused_body(): pl.pallas_call(functools.partial(kernel, frames), out_shape=(pltpu.VMEM(f...]
where the time goes in v3:
time: 15.1 us; the launch traced here: 15 us
  Pallas kernels  14.3 us (95%)
  between operations  0.64 us (4%)
    pallas_call x1, Pallas kernels, fused_body(): pl.pallas_call(functools.partial(kernel, frames), out_shape=(pltpu.VMEM(f...  13.6 us
    pallas_call x1, Pallas kernels, fused_body(): pl.pallas_call(put_out, out_shape=tuple((jax.ShapeDtypeStruct(x.shape, x....  0.66 us

profile of v3, /device:TPU:9, one launch (start us, length us, event | category | flops | bytes accessed | tf_op | source)
XLA Modules:
  0.0 15.0 jit_solution(644652710936327050)
XLA Ops:
  0.6 13.6 %shard_map.157 = (bf16[1,8,16,256]{3,2,1,0:T(8,128)(2,1)S(1)}, bf16[1,8,1024]{2,1,0:T(8,128)(2,1)S(1)}, bf16[1,256]{1,0:T(2,128)(2,1)S(1)}) custom-call(bf16[1,8,16,256]{3,2,1,0:T(8,128)(2,1)} %features.1, s32[1,8,16]{2,1,0:T(8,128)} %masks_in.1, bf16[256]{0:T(256)(128)(2,1)} %mask_embed_in.1, bf16[3,64]{1,0:T(4,128)(2,1)} %mem_tpos_in.1, ...), custom_call_target="tpu_custom_call" | custom-call | tf_op jit(solution)/shard_map/pallas_call | solution.py:588
  14.3 0.7 %shard_map.158 = (bf16[1,8,16,256]{3,2,1,0:T(8,128)(2,1)}, bf16[1,8,1024]{2,1,0:T(8,128)(2,1)}, bf16[1,256]{1,0:T(2,128)(2,1)}) custom-call(bf16[1,8,16,256]{3,2,1,0:T(8,128)(2,1)S(1)} %get-tuple-element.6.refs_0_, bf16[1,8,1024]{2,1,0:T(8,128)(2,1)S(1)} %get-tuple-element.7.refs_1_, bf16[1,256]{1,0:T(2,128)(2,1)S(1)} %get-tuple-element.8.refs_2_), custom_call_target="tpu_custom_call" | custom-call | tf_op jit(solution)/shard_map/pallas_call | solution.py:651

commit v4 on v3

--- a/solution.py
+++ b/solution.py
@@ -13,6 +13,10 @@
 MESH = pl.DeviceIdType.MESH
 F32 = jnp.float32
 BF16 = jnp.bfloat16
+
+
+def stride_of(frames):
+    return max(k for k in range(1, frames + 1) if frames % k == 0 and k * k <= frames)
 
 
 def mm(a, b):
@@ -60,8 +64,7 @@
     halo,
     conv,
     part,
-    part_near,
-    parts_in,
+    table,
     mem_rows,
     mem_send,
     edge_send,
@@ -75,6 +78,8 @@
     edge_recv_sem,
     part_send_sem,
     part_recv_sem,
+    row_send_sem,
+    row_recv_sem,
 ):
     _, rows, columns, dim = features.shape
     tokens = rows * columns
@@ -84,7 +89,15 @@
     t = lax.axis_index("tm")
     s = lax.axis_index("space")
     other = 1 - s
-    reach = min(POINTERS, frames - 1)
+    group = stride_of(frames)
+    stripes = frames // group
+    place, stripe = t % group, t // group
+    fan = {}
+    for offset in range(1 - frames, frames):
+        if 1 <= offset <= MEMS or 0 < abs(offset) < group:
+            fan[offset] = 2
+        elif offset > 0 and offset % group == 0:
+            fan[offset] = 1
     mem_reach = min(MEMS, frames - 1)
 
     loads = []
@@ -113,12 +126,15 @@
     proj_load = load(w_proj, projw)
 
     barrier = pltpu.get_barrier_semaphore()
-    for d in range(reach, 0, -1):
-
-        @pl.when(t - d >= 0)
-        def _(d=d):
-            for to in range(2):
-                pl.semaphore_signal(barrier, inc=1, device_id=(t - d, to), device_id_type=MESH)
+    for offset in sorted(fan, reverse=True):
+        inside = (place - offset >= 0) & (place - offset < group)
+
+        @pl.when(t - offset >= 0 if offset > 0 and (offset <= MEMS or offset >= group) else inside)
+        def _(offset=offset):
+            for to in range(2) if fan[offset] == 2 else (s,):
+                pl.semaphore_signal(
+                    barrier, inc=1, device_id=(t - offset, to), device_id_type=MESH
+                )
 
     pl.semaphore_signal(barrier, inc=1, device_id=(t, other), device_id_type=MESH)
 
@@ -134,11 +150,11 @@
         def _(d=d):
             mem_in[d - 1] = jnp.zeros((2, half, 2 * mem_dim), BF16)
 
-    for d in range(1, POINTERS + 1):
-
-        @pl.when(t - d < 0)
-        def _(d=d):
-            parts_in[d - 1] = jnp.zeros((2, 1, dim), F32)
+    for k in range(1, stripes):
+
+        @pl.when(k > stripe)
+        def _(k=k):
+            table[s, place, k] = jnp.zeros((1, dim), F32)
 
     mask_load.wait()
     mask_f = masks[0].astype(F32)
@@ -153,7 +169,9 @@
     feat_load.wait()
     flat = feat[...].reshape(tokens, dim)
     flat_f = flat.astype(F32)
-    part[...] = jnp.sum(mask_col * flat_f, axis=0, keepdims=True)
+    pooled_part = jnp.sum(mask_col * flat_f, axis=0, keepdims=True)
+    part[...] = pooled_part
+    table[s, place, stripe] = pooled_part
     pix_load.wait()
     embed_load.wait()
     joined_rows = (
@@ -196,8 +214,13 @@
     query = (mm(query_in, queryw[...]) * dim ** (-0.5)).astype(BF16)
     ptr_load.wait()
     peers = 1
-    for d in range(1, reach + 1):
-        peers = peers + (1 - (t + d) // frames) * 2
+    for offset, cores in fan.items():
+        if offset > 0 and (offset <= MEMS or offset >= group):
+            peers = peers + (1 - (t + offset) // frames) * cores
+        elif offset > 0:
+            peers = peers + (1 - (place + offset) // group) * cores
+        else:
+            peers = peers + ((place + offset + group) // group) * cores
     pl.semaphore_wait(barrier, peers)
 
     def send(src, dst, send_sem, recv_sem, frame, to):
@@ -210,14 +233,25 @@
             device_id_type=MESH,
         )
 
-    def part_copy(d, band, to):
+    def stripe_copy(hop, k):
         return send(
             part,
-            parts_in.at[d - 1, band],
-            part_send_sem.at[d - 1, to],
-            part_recv_sem.at[d - 1, band],
-            t + d,
-            to,
+            table.at[s, place, k],
+            part_send_sem.at[hop],
+            part_recv_sem.at[k],
+            t + hop * group,
+            s,
+        )
+
+    def row_copy(shift, band, to):
+        at = table.at[band, (place - shift + group) % group if to is None else place]
+        return send(
+            at,
+            at,
+            row_send_sem.at[shift, band if to is None else to],
+            row_recv_sem.at[shift, band],
+            stripe * group + (place + shift) % group,
+            other if to is None else to,
         )
 
     main = half - columns
@@ -247,15 +281,14 @@
     edge_at = pl.multiple_of(other * (tokens - columns), columns)
     edge_rows = pl.ds(edge_at, columns)
     halo_copy = send(
-        joined.at[1 + other * (rows - 1)], halo, near_send.at[1], near_recv.at[1], t, other
+        joined.at[1 + other * (rows - 1)], halo, near_send, near_recv, t, other
     )
     halo_copy.start()
-    for d in range(reach, 0, -1):
-
-        @pl.when(t + d < frames)
-        def _(d=d):
-            for to in range(2):
-                part_copy(d, s, to).start()
+    for hop in range(stripes - 1, 0, -1):
+
+        @pl.when(t + hop * group < frames)
+        def _(hop=hop):
+            stripe_copy(hop, stripe).start()
 
     for d in range(mem_reach, 0, -1):
 
@@ -263,9 +296,6 @@
         def _(d=d):
             for to in range(2):
                 main_copy(d, s, to).start()
-
-    near_copy = send(part, part_near, near_send.at[0], near_recv.at[0], t, other)
-    near_copy.start()
 
     key_load.wait()
     value_load.wait()
@@ -280,13 +310,28 @@
             [pointer_rows[:, j * mem_dim : (j + 1) * mem_dim] for j in range(parts)], axis=0
         )
 
-    ptr_tokens = parts * POINTERS
-    ptr_tpos_keys = mm(cut(ptr_tpos[...]), key_w)
+    ptr_tokens = parts * frames
+    row_id = lax.broadcasted_iota(jnp.int32, (frames, POINTERS), 0)
+    row_age = t - 1 - ((row_id % stripes) * group + row_id // stripes)
+    pick = row_age == lax.broadcasted_iota(jnp.int32, (frames, POINTERS), 1)
+    aged_tpos = mm(jnp.where(pick, 1.0, 0.0).astype(BF16), ptr_tpos[...]).astype(BF16)
+    ptr_tpos_keys = mm(cut(aged_tpos), key_w)
     null_rows = jnp.broadcast_to(
         empty_memory[...].astype(F32).reshape(1, mem_dim), (ptr_tokens, mem_dim)
     ).astype(BF16)
     null_keys = mm(null_rows, key_w).astype(BF16)
     null_values = mm(null_rows, value_w).astype(BF16)
+
+    def relay():
+        for k in range(stripes - 1):
+
+            @pl.when(k < stripe)
+            def _(k=k):
+                stripe_copy(1, k).wait_recv()
+
+        for shift in range(group - 1, -1, -1):
+            for to in range(2) if shift else (other,):
+                row_copy(shift, s, to).start()
 
     halo_copy.wait()
     tap = 2 * other
@@ -303,6 +348,7 @@
                 edge_copy(d, s, to).start()
 
     mem_rows[edge_rows] = edge_twice
+    relay()
     for c in range(0, columns, 2):
         even = mem_rows[pl.ds(c, rows, stride=columns), :]
         odd = mem_rows[pl.ds(c + 1, rows, stride=columns), :]
@@ -314,9 +360,6 @@
         normed = pooled * lax.rsqrt(jnp.mean(pooled * pooled, axis=1, keepdims=True) + 1e-06)
         return mm(normed.astype(BF16), ptrw[...]).astype(BF16)
 
-    near_copy.wait()
-    pointers[...] = to_pointers(jnp.broadcast_to(part[...] + part_near[...], (8, dim)))[0:1]
-
     key_low, key_high = key_pad[mem_dim : 3 * mem_dim], key_pad[0 : 2 * mem_dim]
     value_low, value_high = value_pad[mem_dim : 3 * mem_dim], value_pad[0 : 2 * mem_dim]
 
@@ -340,21 +383,23 @@
         return block(jnp.concatenate(keys, axis=0), jnp.concatenate(vals, axis=0), t - d >= 0)
 
     def pointer_block():
-        for d in range(1, reach + 1):
-
-            @pl.when(t - d >= 0)
-            def _(d=d):
-                for band in range(2):
-                    part_copy(d, band, other).wait_recv()
-
-        tokens_in = cut(to_pointers((parts_in[:, 0] + parts_in[:, 1]).reshape(POINTERS, dim)))
+        for shift in range(group):
+            for band in range(2) if shift else (other,):
+                row_copy(shift, band, None).wait_recv()
+
+        own = table[0, place, stripe] + table[1, place, stripe]
+        pointers[...] = to_pointers(jnp.broadcast_to(own, (8, dim)))[0:1]
+        pooled = (table[0] + table[1]).reshape(frames, dim)
+        tokens_in = cut(to_pointers(pooled))
         keys = jnp.concatenate(
             [(mm(tokens_in, key_w) + ptr_tpos_keys).astype(BF16), null_keys], axis=0
         )
         vals = jnp.concatenate([mm(tokens_in, value_w).astype(BF16), null_values], axis=0)
         index = lax.broadcasted_iota(jnp.int32, (1, 2 * ptr_tokens), 1)
-        oldest = t - 1 - index % POINTERS
-        valid = ((index < ptr_tokens) & (oldest >= 0)) | (index == ptr_tokens)
+        row = index % frames
+        age = t - 1 - ((row % stripes) * group + row // stripes)
+        known = (age >= 0) & (age < POINTERS)
+        valid = ((index < ptr_tokens) & known) | (index == ptr_tokens)
         return block(keys, vals, valid)
 
     blocks = [pointer_block() if d == 0 else memory_block(d) for d in BLOCK_ORDER]
@@ -367,15 +412,23 @@
     result = feat[...].reshape(tokens, dim).astype(F32) + mm(mixed, projw[...])
     attended[0] = result.astype(BF16).reshape(rows, columns, dim)
 
-    for d in range(1, reach + 1):
+    for hop in range(1, stripes):
+
+        @pl.when(t + hop * group < frames)
+        def _(hop=hop):
+            stripe_copy(hop, stripe).wait_send()
+
+    for shift in range(group):
+        for to in range(2) if shift else (other,):
+            row_copy(shift, s, to).wait_send()
+
+    for d in range(1, mem_reach + 1):
 
         @pl.when(t + d < frames)
         def _(d=d):
             for to in range(2):
-                part_copy(d, s, to).wait_send()
-                if d <= mem_reach:
-                    main_copy(d, s, to).wait_send()
-                    edge_copy(d, s, to).wait_send()
+                main_copy(d, s, to).wait_send()
+                edge_copy(d, s, to).wait_send()
 
 
 def from_behind(block, axis, distance):
@@ -582,6 +635,7 @@
     mem_dim = w_key.shape[0]
     tokens = rows * columns
     half = tokens // 2
+    group = stride_of(frames)
     vmem = pl.BlockSpec(memory_space=pltpu.VMEM)
     hbm = pl.BlockSpec(memory_space=pltpu.HBM)
     dma = pltpu.SemaphoreType.DMA
@@ -613,21 +667,22 @@
             pltpu.VMEM((columns, dim), BF16),
             pltpu.VMEM((tokens, dim), F32),
             pltpu.VMEM((1, dim), F32),
-            pltpu.VMEM((1, dim), F32),
-            pltpu.VMEM((POINTERS, 2, 1, dim), F32),
+            pltpu.VMEM((2, group, frames // group, 1, dim), F32),
             pltpu.VMEM((tokens, 2 * mem_dim), F32),
             pltpu.VMEM((half, 2 * mem_dim), BF16),
             pltpu.VMEM((columns, 2 * mem_dim), BF16),
             pltpu.VMEM((MEMS, 2, half, 2 * mem_dim), BF16),
             dma((17,)),
-            dma((2,)),
-            dma((2,)),
+            dma,
+            dma,
             dma((MEMS, 2)),
             dma((MEMS, 2)),
             dma((MEMS, 2)),
             dma((MEMS, 2)),
-            dma((POINTERS, 2)),
-            dma((POINTERS, 2)),
+            dma((frames // group,)),
+            dma((frames // group,)),
+            dma((group, 2)),
+            dma((group, 2)),
         ],
         compiler_params=pltpu.CompilerParams(
             collective_id=0, has_side_effects=True
@@ -662,6 +717,7 @@
     frames_dev, rows, columns, dim = features.shape
     key_count = MEMS * 2 * rows * columns
     fits = rows * columns * key_count * 4 <= 2**23 and rows * columns <= 256
+    fits = fits and stride_of(lax.axis_size("tm")) > MEMS
     if frames_dev == 1 and lax.axis_size("space") == 2 and fits:
         return fused_body(features, *rest)
     return staged_body(features, *rest)

time: 15.1 us -> 14 us (0.927)
  Pallas kernels: 14.3 us -> 13.1 us
    pallas_call x1, Pallas kernels: 13.6 us -> 12.5 us  [fused_body(): pl.pallas_call(functools.partial(kernel, frames), out_shape=(pltpu.VMEM(f...]
where the time goes in v4:
time: 14 us; the launch traced here: 13.8 us
  Pallas kernels  13.1 us (94%)
  between operations  0.64 us (5%)
    pallas_call x1, Pallas kernels, fused_body(): pl.pallas_call(functools.partial(kernel, frames), out_shape=(pltpu.VMEM(f...  12.5 us
    pallas_call x1, Pallas kernels, fused_body(): pl.pallas_call(put_out, out_shape=tuple((jax.ShapeDtypeStruct(x.shape, x....  0.66 us

profile of v4, /device:TPU:9, one launch (start us, length us, event | category | flops | bytes accessed | tf_op | source)
XLA Modules:
  0.0 13.8 jit_solution(4717311145859595223)
XLA Ops:
  0.6 12.5 %shard_map.157 = (bf16[1,8,16,256]{3,2,1,0:T(8,128)(2,1)S(1)}, bf16[1,8,1024]{2,1,0:T(8,128)(2,1)S(1)}, bf16[1,256]{1,0:T(2,128)(2,1)S(1)}) custom-call(bf16[1,8,16,256]{3,2,1,0:T(8,128)(2,1)} %features.1, s32[1,8,16]{2,1,0:T(8,128)} %masks_in.1, bf16[256]{0:T(256)(128)(2,1)} %mask_embed_in.1, bf16[3,64]{1,0:T(4,128)(2,1)} %mem_tpos_in.1, ...), custom_call_target="tpu_custom_call" | custom-call | tf_op jit(solution)/shard_map/pallas_call | solution.py:642
  13.1 0.7 %shard_map.158 = (bf16[1,8,16,256]{3,2,1,0:T(8,128)(2,1)}, bf16[1,8,1024]{2,1,0:T(8,128)(2,1)}, bf16[1,256]{1,0:T(2,128)(2,1)}) custom-call(bf16[1,8,16,256]{3,2,1,0:T(8,128)(2,1)S(1)} %get-tuple-element.6.refs_0_, bf16[1,8,1024]{2,1,0:T(8,128)(2,1)S(1)} %get-tuple-element.7.refs_1_, bf16[1,256]{1,0:T(2,128)(2,1)S(1)} %get-tuple-element.8.refs_2_), custom_call_target="tpu_custom_call" | custom-call | tf_op jit(solution)/shard_map/pallas_call | solution.py:706
